TPU v7x, 256 devices: a whole 4x4x8 slice. The times are simulated.
256 devices in a mesh: seq: 32 (over x, z), mlp: 8 (over y, core).
Axes of the slice: x: 4, y: 4, z: 8, core: 2. Of those that a mesh axis runs over, the one named last changes fastest.
Arguments:
- queries: bfloat16 [1024, 2560], P(('seq', 'mlp')), may hold values from -8 to 8
- new_kv: bfloat16 [1024, 512], P(('seq', 'mlp')), may hold values from -5 to 5
- kv_cache: bfloat16 [4352, 128, 512], P(('seq', 'mlp')), may hold values from -4 to 4, as said below
- lengths: int32 [256], replicated, may hold values from 256 to 16384, as said below
- page_table: int32 [256, 128], replicated, may hold values from -1 to 4351, as said below
- residual: bfloat16 [1024, 2560], P('seq', 'mlp'), may hold values from -3 to 3
- out_weight: bfloat16 [2560, 2560], P(None, 'mlp'), may hold values from -0.125 to 0.125
- norm_gain: float32 [2560], replicated, may hold values from 0.1 to 1.9
- gate_weight: bfloat16 [2560, 3840], P(None, 'mlp'), may hold values from -0.125 to 0.125
- up_weight: bfloat16 [2560, 3840], P(None, 'mlp'), may hold values from -0.125 to 0.125
- down_weight: bfloat16 [3840, 2560], P('mlp'), may hold values from -0.09375 to 0.09375
- next_gain: float32 [2560], replicated, may hold values from 0.1 to 1.9
- qkv_weight: bfloat16 [2560, 3072], P(None, 'mlp'), may hold values from -0.125 to 0.125
Outputs:
- attended: bfloat16 [1024, 2560], P(('seq', 'mlp'))
- residual_out: bfloat16 [1024, 2560], P('seq', 'mlp')
- next_qkv: bfloat16 [1024, 3072], P('seq', 'mlp')
Inputs may be any that keep to these rules, and one draw needn't show every extreme that they name: `lengths`: lengths have a heavy tail; at least one request has exactly 16384. page_table[r, p] is a slot exactly for the pages p holding positions max(0, lengths[r] - 2047) to lengths[r] - 1, and -1 elsewhere. Slots d * 17 to d * 17 + 16 lie on device d of seq+mlp. All pages of request r lie in consecutive slots of ONE device, whose mlp index is r modulo 8; a device may hold the pages of several requests or of none. No slot holds two pages; some device of every mlp index has all 17 slots in use. `kv_cache`: unused slots hold arbitrary values.
All inputs are finite; a program needn't handle non-finite values.
Results may differ from a plain program's by a relative error of at most 0.011.
Values may be sent and summed in bfloat16 or wider, within the bound.
No kernel may reach another device: no remote copies, remote signals or barrier semaphores. Data moves between devices by JAX's collectives and lax.ppermute only.
A program may use at most 64 MiB of HBM per device.

v0:
```python
import jax
import jax.numpy as jnp
from jax import lax
from jax.sharding import PartitionSpec as P

WINDOW = 2048
NEG_FILL = -1e30


def combine_parts(first, second):
    first_max, first_sum, first_acc = first
    second_max, second_sum, second_acc = second
    peak = jnp.maximum(first_max, second_max)
    first_factor = jnp.exp(first_max - peak)
    second_factor = jnp.exp(second_max - peak)
    return (
        peak,
        first_sum * first_factor + second_sum * second_factor,
        first_acc * first_factor[..., None] + second_acc * second_factor[..., None],
    )


def rms_norm(values, gain):
    floats = values.astype(jnp.float32)
    scaled = floats * lax.rsqrt(jnp.mean(floats * floats, axis=-1, keepdims=True) + 1e-06)
    return (scaled * gain).astype(jnp.bfloat16)


def shards(
    queries,
    new_kv,
    kv_cache,
    lengths,
    page_table,
    residual,
    out_weight,
    norm_gain,
    gate_weight,
    up_weight,
    down_weight,
    next_gain,
    qkv_weight,
):
    seq_count = lax.axis_size("seq")
    mlp_count = lax.axis_size("mlp")
    seq_place = lax.axis_index("seq")
    device = seq_place * mlp_count + lax.axis_index("mlp")
    slot_count = kv_cache.shape[0]
    page_len = kv_cache.shape[1]
    head_dim = kv_cache.shape[2] // 2
    token_count = queries.shape[0]
    width = queries.shape[1]
    head_count = width // head_dim
    request_total, page_count = page_table.shape
    scale = head_dim ** (-0.5)
    local_slot = page_table - device * slot_count
    inside = (local_slot >= 0) & (local_slot < slot_count)
    target = jnp.where(inside, local_slot, slot_count).reshape(-1)
    owners = jnp.broadcast_to(
        jnp.arange(request_total, dtype=jnp.int32)[:, None], page_table.shape
    ).reshape(-1)
    page_numbers = jnp.broadcast_to(
        jnp.arange(page_count, dtype=jnp.int32)[None, :], page_table.shape
    ).reshape(-1)
    slot_request = jnp.zeros((slot_count,), jnp.int32).at[target].set(owners, mode="drop")
    slot_page = jnp.zeros((slot_count,), jnp.int32).at[target].set(page_numbers, mode="drop")
    slot_used = jnp.zeros((slot_count,), jnp.bool_).at[target].set(True, mode="drop")
    column_rows = lax.all_gather(queries, "seq", axis=0, tiled=True)
    column_queries = column_rows.reshape(seq_count, token_count, head_count, head_dim)
    slot_column = slot_request // mlp_count
    slot_queries = column_queries[slot_column]
    cache_keys = kv_cache[:, :, :head_dim]
    cache_values = kv_cache[:, :, head_dim:]
    scores = (
        jnp.einsum("sqhd,skd->sqhk", slot_queries, cache_keys, preferred_element_type=jnp.float32)
        * scale
    )
    positions = slot_page[:, None] * page_len + jnp.arange(page_len, dtype=jnp.int32)[None, :]
    slot_length = lengths[slot_request]
    offsets = jnp.arange(token_count, dtype=jnp.int32)
    valid = (
        slot_used[:, None, None]
        & (positions[:, None, :] < slot_length[:, None, None])
        & (
            positions[:, None, :]
            >= slot_length[:, None, None] + offsets[None, :, None] - (WINDOW - 1)
        )
    )
    valid = valid[:, :, None, :]
    page_max = jnp.max(jnp.where(valid, scores, NEG_FILL), axis=-1)
    weights = jnp.where(valid, jnp.exp(scores - page_max[..., None]), 0.0)
    page_sum = jnp.sum(weights, axis=-1)
    page_acc = jnp.einsum(
        "sqhk,skd->sqhd",
        weights.astype(jnp.bfloat16),
        cache_values,
        preferred_element_type=jnp.float32,
    )
    member = (slot_column[None, :] == jnp.arange(seq_count, dtype=jnp.int32)[:, None]) & slot_used[
        None, :
    ]
    request_max = jnp.max(jnp.where(member[:, :, None, None], page_max[None], NEG_FILL), axis=1)
    rescale = jnp.exp(page_max - request_max[slot_column])
    member_float = member.astype(jnp.float32)
    request_sum = jnp.einsum(
        "rs,sqh->rqh", member_float, rescale * page_sum, precision=lax.Precision.HIGHEST
    )
    request_acc = jnp.einsum(
        "rs,sqhd->rqhd",
        member_float,
        rescale[..., None] * page_acc,
        precision=lax.Precision.HIGHEST,
    )
    got_max, got_sum, got_acc = (
        lax.all_to_all(request_max, "seq", split_axis=0, concat_axis=0, tiled=True),
        lax.all_to_all(request_sum, "seq", split_axis=0, concat_axis=0, tiled=True),
        lax.all_to_all(request_acc, "seq", split_axis=0, concat_axis=0, tiled=True),
    )
    peak = jnp.max(got_max, axis=0)
    factor = jnp.exp(got_max - peak[None])
    own_part = (
        peak,
        jnp.sum(factor * got_sum, axis=0),
        jnp.sum(factor[..., None] * got_acc, axis=0),
    )
    own_queries = queries.reshape(token_count, head_count, head_dim)
    new_keys = new_kv[:, :head_dim]
    new_values = new_kv[:, head_dim:]
    new_scores = (
        jnp.einsum("qhd,kd->qhk", own_queries, new_keys, preferred_element_type=jnp.float32) * scale
    )
    causal = (offsets[:, None] >= offsets[None, :])[:, None, :]
    new_max = jnp.max(jnp.where(causal, new_scores, NEG_FILL), axis=-1)
    new_weights = jnp.where(causal, jnp.exp(new_scores - new_max[..., None]), 0.0)
    new_sum = jnp.sum(new_weights, axis=-1)
    new_acc = jnp.einsum(
        "qhk,kd->qhd",
        new_weights.astype(jnp.bfloat16),
        new_values,
        preferred_element_type=jnp.float32,
    )
    final_max, final_sum, final_acc = combine_parts(own_part, (new_max, new_sum, new_acc))
    attended = (final_acc / final_sum[..., None]).reshape(token_count, width).astype(jnp.bfloat16)
    attention_out = jnp.dot(
        lax.all_gather(attended, "mlp", axis=0, tiled=True),
        out_weight,
        preferred_element_type=jnp.float32,
    )
    stream = (residual.astype(jnp.float32) + attention_out).astype(jnp.bfloat16)
    whole_stream = lax.all_gather(stream, "mlp", axis=1, tiled=True)
    normed = rms_norm(whole_stream, norm_gain)
    gate = jnp.dot(normed, gate_weight, preferred_element_type=jnp.float32)
    upward = jnp.dot(normed, up_weight, preferred_element_type=jnp.float32)
    hidden = (jax.nn.gelu(gate, approximate=True) * upward).astype(jnp.bfloat16)
    partial_down = jnp.dot(hidden, down_weight, preferred_element_type=jnp.float32)
    column_width = stream.shape[1]
    column_start = lax.axis_index("mlp") * column_width
    down_total = lax.psum(partial_down, "mlp")
    full_after = (whole_stream.astype(jnp.float32) + down_total).astype(jnp.bfloat16)
    shard_after = lax.dynamic_slice_in_dim(full_after, column_start, column_width, 1)
    normed_next = rms_norm(full_after, next_gain)
    next_qkv = jnp.dot(normed_next, qkv_weight, preferred_element_type=jnp.float32).astype(
        jnp.bfloat16
    )
    return (attended, shard_after, next_qkv)


def solution(mesh):
    return jax.shard_map(
        shards,
        mesh=mesh,
        in_specs=(
            P(("seq", "mlp"), None),
            P(("seq", "mlp"), None),
            P(("seq", "mlp"), None, None),
            P(),
            P(),
            P("seq", "mlp"),
            P(None, "mlp"),
            P(),
            P(None, "mlp"),
            P(None, "mlp"),
            P("mlp", None),
            P(),
            P(None, "mlp"),
        ),
        out_specs=(P(("seq", "mlp"), None), P("seq", "mlp"), P("seq", "mlp")),
        check_vma=False,
    )
```

profile of v0, /device:TPU:2, one launch (start us, length us, event | category | flops | bytes accessed | tf_op | source)
XLA Modules:
  0.0 617.3 jit_solution(3208878940347870312)
XLA Ops:
  8.5 120.0 %scatter_custom_fusion = s32[17]{0:T(128)S(1)} fusion(s32[32768]{0:T(1024)S(1)} %bitcast.70, s32[32768]{0:T(1024)S(1)} %iota_bitcast_fusion.1, s32[]{:T(128)} %constant.28.clone.1), kind=kCustom, calls=%fused_computation.111 | custom fusion | bytes 72 | tf_op jit(solution)/shard_map/scatter | solution.py:65
  130.0 120.0 %scatter_custom_fusion.2 = s32[17]{0:T(128)S(1)} fusion(s32[32768]{0:T(1024)S(1)} %bitcast.71, s32[32768]{0:T(1024)S(1)} %iota_bitcast_fusion, s32[]{:T(128)} %constant.28.clone.1), kind=kCustom, calls=%fused_computation.109 | custom fusion | bytes 72 | tf_op jit(solution)/shard_map/scatter | solution.py:66
  250.1 136.5 %scatter_custom_fusion.1 = pred[17]{0:T(512)(128)(4,1)S(1)} fusion(s32[32768]{0:T(1024)S(1)} %bitcast.72, pred[32768]{0:T(1024)(128)(4,1)S(1)} %broadcast.184, pred[]{:T(512)} %constant.20.clone.1), kind=kCustom, calls=%fused_computation.104 | custom fusion | bytes 18 | tf_op jit(solution)/shard_map/scatter | solution.py:67
  386.7 52.5 %all-gather = bf16[32,4,2560]{2,1,0:T(4,128)(2,1)S(1)} all-gather(bf16[1,4,2560]{2,1,0:T(4,128)(2,1)} %bitcast.74), channel_id=1, replica_groups=mesh['seq'=32,'mlp'=8] {'seq'}, dimensions={0}, use_global_device_ids=true | all-gather | bytes 675840 | tf_op jit(solution)/shard_map/all_gather | solution.py:68
  440.7 2.7 gather_fusion.1
  443.4 2.0 select_reduce_fusion
  447.2 1.4 gather_fusion.2
  449.6 6.7 %all-to-all-start.2 = ((f32[32,4,10]{2,1,0:T(4,128)}), f32[32,4,10]{2,1,0:T(4,128)S(1)}, u32[]{:S(2)}, u32[]{:S(2)}) async-start(f32[32,4,10]{2,1,0:T(4,128)} %copy.58), calls=%async_computation.2 | async-start | bytes 131072 | tf_op jit(solution)/shard_map/all_to_all | solution.py:116
  456.3 2.7 convolution_multiply_fusion
  459.0 6.5 %all-to-all-done.2 = f32[32,4,10]{2,1,0:T(4,128)S(1)} async-done(((f32[32,4,10]{2,1,0:T(4,128)}), f32[32,4,10]{2,1,0:T(4,128)S(1)}, u32[]{:S(2)}, u32[]{:S(2)}) %all-to-all-start.2) | async-done | bytes 5152 | tf_op jit(solution)/shard_map/all_to_all | solution.py:116
  465.4 5.0 all-to-all-start
  470.4 2.3 fusion.11
  472.7 1.9 copy.55
  474.6 4.9 all-to-all-done
  479.6 6.7 %all-to-all-start.1 = ((f32[32,4,10,256]{3,1,2,0:T(4,128)}), f32[32,4,10,256]{3,1,2,0:T(4,128)}, u32[]{:S(2)}, u32[]{:S(2)}) async-start(f32[32,4,10,256]{3,1,2,0:T(4,128)} %copy.55), calls=%async_computation.1 | async-start | bytes 2621440 | tf_op jit(solution)/shard_map/all_to_all | solution.py:117
  487.1 18.4 %all-to-all-done.1 = f32[32,4,10,256]{3,1,2,0:T(4,128)} async-done(((f32[32,4,10,256]{3,1,2,0:T(4,128)}), f32[32,4,10,256]{3,1,2,0:T(4,128)}, u32[]{:S(2)}, u32[]{:S(2)}) %all-to-all-start.1) | async-done | bytes 1310752 | tf_op jit(solution)/shard_map/all_to_all | solution.py:117
  505.4 1.7 multiply_reduce_fusion
  507.4 13.3 %all-gather.1 = bf16[8,4,2560]{2,1,0:T(4,128)(2,1)S(1)} all-gather(bf16[1,4,2560]{2,1,0:T(4,128)(2,1)S(1)} %reshape.292), channel_id=1, replica_groups=mesh['seq'=32,'mlp'=8] {'mlp'}, dimensions={0}, use_global_device_ids=true | all-gather | bytes 184320 | tf_op jit(solution)/shard_map/all_gather | solution.py:145
  520.8 2.0 fusion.10
  522.8 12.8 %all-gather.2 = bf16[8,320,32]{1,2,0:T(8,128)(2,1)S(1)} all-gather(bf16[1,320,32]{1,2,0:T(8,128)(2,1)S(1)} %fusion.10), channel_id=1, replica_groups=mesh['seq'=32,'mlp'=8] {'mlp'}, dimensions={0}, use_global_device_ids=true | all-gather | bytes 184320 | tf_op jit(solution)/shard_map/all_gather | solution.py:150
  536.0 2.5 fusion.74
  538.5 3.8 fusion.9
  542.9 63.1 %all-reduce.2.cloned.1.call-done = f32[32,2560]{1,0:T(8,128)} async-done(((f32[32,2560]{1,0:T(8,128)}), f32[32,2560]{1,0:T(8,128)}) %all-reduce.2.cloned.1.call-update) | async-done | bytes 327696 | tf_op jit(solution)/shard_map/psum | solution.py:158
  607.9 2.6 convolution_convert_fusion
  (57 shorter events, 11.1 us)
Async XLA Ops:
  7.2 531.3 %copy-start = (bf16[480,2560]{1,0:T(8,128)(2,1)S(1)}, bf16[480,2560]{1,0:T(8,128)(2,1)}, u32[]{:S(2)}) copy-start(bf16[480,2560]{1,0:T(8,128)(2,1)} %param.23) | copy-start | bytes 7372804
  449.6 15.8 %all-to-all-start.2 = ((f32[32,4,10]{2,1,0:T(4,128)}), f32[32,4,10]{2,1,0:T(4,128)S(1)}, u32[]{:S(2)}, u32[]{:S(2)}) async-start(f32[32,4,10]{2,1,0:T(4,128)} %copy.58), calls=%async_computation.2 | async-start | bytes 131072 | tf_op jit(solution)/shard_map/all_to_all | solution.py:116
  465.4 14.2 %all-to-all-start = ((f32[32,4,10]{2,1,0:T(4,128)}), f32[32,4,10]{2,1,0:T(4,128)S(1)}, u32[]{:S(2)}, u32[]{:S(2)}) async-start(f32[32,4,10]{2,1,0:T(4,128)} %copy.51), calls=%async_computation | async-start | bytes 131072 | tf_op jit(solution)/shard_map/all_to_all | solution.py:115
  474.6 11.7 %copy-start.1 = (bf16[4,2560]{1,0:T(4,128)(2,1)S(1)}, bf16[4,2560]{1,0:T(4,128)(2,1)}, u32[]{:S(2)}) copy-start(bf16[4,2560]{1,0:T(4,128)(2,1)} %param.13) | copy-start | bytes 61444
  474.6 11.7 %copy-start.5 = (bf16[4,512]{1,0:T(4,128)(2,1)S(1)}, bf16[4,512]{1,0:T(4,128)(2,1)}, u32[]{:S(2)}) copy-start(bf16[4,512]{1,0:T(4,128)(2,1)} %param.14) | copy-start | bytes 12292
  479.6 25.8 %all-to-all-start.1 = ((f32[32,4,10,256]{3,1,2,0:T(4,128)}), f32[32,4,10,256]{3,1,2,0:T(4,128)}, u32[]{:S(2)}, u32[]{:S(2)}) async-start(f32[32,4,10,256]{3,1,2,0:T(4,128)} %copy.55), calls=%async_computation.1 | async-start | bytes 2621440 | tf_op jit(solution)/shard_map/all_to_all | solution.py:117
  486.3 34.5 %copy-start.3 = (bf16[32,320]{1,0:T(8,128)(2,1)S(1)}, bf16[32,320]{1,0:T(8,128)(2,1)}, u32[]{:S(2)}) copy-start(bf16[32,320]{1,0:T(8,128)(2,1)} %param.18) | copy-start | bytes 61444
  486.3 119.8 %all-reduce.2.cloned.1.call-start = ((), (), s32[]{:S(2)}) async-start(), calls=%async_computation.3 | async-start | bytes 655360 | tf_op jit(solution)/shard_map/psum | solution.py:158
  520.7 15.2 %copy-start.2 = (f32[2560]{0:T(1024)S(1)}, f32[2560]{0:T(1024)}, u32[]{:S(2)}) copy-start(f32[2560]{0:T(1024)} %param.20) | copy-start | bytes 30724
  538.4 69.4 %copy-start.4 = (f32[2560]{0:T(1024)S(1)}, f32[2560]{0:T(1024)}, u32[]{:S(2)}) copy-start(f32[2560]{0:T(1024)} %param.24) | copy-start | bytes 30724
Sparse Core Ops, SparseCore 0:
  542.4 63.6 all-reduce.1
where the time goes:
time: 618 us; the launch traced here: 617 us
  local copies, waits for them, and re-layouts  389 us (63%)
  waiting for transfers between devices  92.9 us (15%)
  blocking collectives  78.6 us (13%)
  matrix products  18.6 us (3%)
  starting transfers between devices  18.3 us (3%)
  between operations  14.3 us (2%)
    scatter x1, local copies, waits for them, and re-layouts, shards(): jnp.zeros((slot_count,), jnp.bool_).at[target].set(True, mode='drop')  136 us
    scatter x1, local copies, waits for them, and re-layouts, shards(): jnp.zeros((slot_count,), jnp.int32).at[target].set(owners, mode='drop')  120 us
    scatter x1, local copies, waits for them, and re-layouts, shards(): jnp.zeros((slot_count,), jnp.int32).at[target]  120 us
    psum x1, waiting for transfers between devices, shards(): down_total = lax.psum(partial_down, 'mlp')  63.1 us
    all_gather x1, blocking collectives, shards(): column_rows = lax.all_gather(queries, 'seq', axis=0, tiled=True)  52.5 us
    all_to_all x1, waiting for transfers between devices, shards(): lax.all_to_all(request_acc, 'seq', split_axis=0, concat_axis=0, tiled=True)  18.4 us
    all_gather x1, blocking collectives, shards(): lax.all_gather(attended, 'mlp', axis=0, tiled=True)  13.3 us
    all_gather x1, blocking collectives, shards(): whole_stream = lax.all_gather(stream, 'mlp', axis=1, tiled=True)  12.8 us
  transfers between devices with their start and end apart: 4, of which 4 were waited for; matrix products, arithmetic and copies ran while one was open for 1% of the time, Pallas kernels for 0%

commit v1 on v0

--- a/solution.py
+++ b/solution.py
@@ -155,7 +155,13 @@
     partial_down = jnp.dot(hidden, down_weight, preferred_element_type=jnp.float32)
     column_width = stream.shape[1]
     column_start = lax.axis_index("mlp") * column_width
-    down_total = lax.psum(partial_down, "mlp")
+    down_total = partial_down
+    dev_count = lax.axis_size("mlp")
+    for kk in [dev_i for dev_i in (1, 2, 4, 8, 16) if dev_i < dev_count]:
+        steps_seen = []
+        for i in range(dev_count):
+            steps_seen.append((i, i ^ kk))
+        down_total = down_total + lax.ppermute(down_total, axis_name="mlp", perm=steps_seen)
     full_after = (whole_stream.astype(jnp.float32) + down_total).astype(jnp.bfloat16)
     shard_after = lax.dynamic_slice_in_dim(full_after, column_start, column_width, 1)
     normed_next = rms_norm(full_after, next_gain)

time: 618 us -> 564 us (0.913)
  waiting for transfers between devices: 92.9 us -> 47.6 us
  between operations: 14.3 us -> 0.91 us
    psum x1 -> x0, waiting for transfers between devices: 63.1 us -> none  [shards(): down_total = lax.psum(partial_down, 'mlp')]
    ppermute x0 -> x3, waiting for transfers between devices: none -> 17.8 us  [shards(): lax.ppermute(down_total, axis_name='mlp', perm=steps_seen)]
  transfers between devices with their start and end apart: 4 -> 6, of which waited for: 4 -> 6; matrix products, arithmetic and copies ran while one was open for 1% -> 1% of each run, Pallas kernels for 0% -> 0%
where the time goes in v1:
time: 564 us; the launch traced here: 561 us
  local copies, waits for them, and re-layouts  389 us (69%)
  blocking collectives  78.6 us (14%)
  waiting for transfers between devices  47.6 us (8%)
  starting transfers between devices  22.3 us (4%)
  matrix products  17.8 us (3%)
    scatter x1, local copies, waits for them, and re-layouts, shards(): jnp.zeros((slot_count,), jnp.bool_).at[target].set(True, mode='drop')  136 us
    scatter x1, local copies, waits for them, and re-layouts, shards(): jnp.zeros((slot_count,), jnp.int32).at[target].set(owners, mode='drop')  120 us
    scatter x1, local copies, waits for them, and re-layouts, shards(): jnp.zeros((slot_count,), jnp.int32).at[target]  120 us
    all_gather x1, blocking collectives, shards(): column_rows = lax.all_gather(queries, 'seq', axis=0, tiled=True)  52.5 us
    all_to_all x1, waiting for transfers between devices, shards(): lax.all_to_all(request_acc, 'seq', split_axis=0, concat_axis=0, tiled=True)  18.4 us
    ppermute x3, waiting for transfers between devices, shards(): lax.ppermute(down_total, axis_name='mlp', perm=steps_seen)  17.8 us
    all_gather x1, blocking collectives, shards(): lax.all_gather(attended, 'mlp', axis=0, tiled=True)  13.3 us
    all_gather x1, blocking collectives, shards(): whole_stream = lax.all_gather(stream, 'mlp', axis=1, tiled=True)  12.8 us
  transfers between devices with their start and end apart: 6, of which 6 were waited for; matrix products, arithmetic and copies ran while one was open for 1% of the time, Pallas kernels for 0%

profile of v1, /device:TPU:2, one launch (start us, length us, event | category | flops | bytes accessed | tf_op | source)
XLA Modules:
  0.0 561.0 jit_solution(3437485846444948376)
XLA Ops:
  1.9 120.0 %scatter_custom_fusion = s32[17]{0:T(128)S(1)} fusion(s32[32768]{0:T(1024)S(1)} %bitcast.70, s32[32768]{0:T(1024)S(1)} %iota_bitcast_fusion.1, s32[]{:T(128)} %constant.28.clone.1), kind=kCustom, calls=%fused_computation.111 | custom fusion | bytes 72 | tf_op jit(solution)/shard_map/scatter | solution.py:65
  123.4 120.0 %scatter_custom_fusion.2 = s32[17]{0:T(128)S(1)} fusion(s32[32768]{0:T(1024)S(1)} %bitcast.71, s32[32768]{0:T(1024)S(1)} %iota_bitcast_fusion, s32[]{:T(128)} %constant.28.clone.1), kind=kCustom, calls=%fused_computation.109 | custom fusion | bytes 72 | tf_op jit(solution)/shard_map/scatter | solution.py:66
  243.6 136.5 %scatter_custom_fusion.1 = pred[17]{0:T(512)(128)(4,1)S(1)} fusion(s32[32768]{0:T(1024)S(1)} %bitcast.72, pred[32768]{0:T(1024)(128)(4,1)S(1)} %broadcast.184, pred[]{:T(512)} %constant.20.clone.1), kind=kCustom, calls=%fused_computation.104 | custom fusion | bytes 18 | tf_op jit(solution)/shard_map/scatter | solution.py:67
  380.1 52.5 %all-gather = bf16[32,4,2560]{2,1,0:T(4,128)(2,1)S(1)} all-gather(bf16[1,4,2560]{2,1,0:T(4,128)(2,1)} %bitcast.74), channel_id=1, replica_groups=mesh['seq'=32,'mlp'=8] {'seq'}, dimensions={0}, use_global_device_ids=true | all-gather | bytes 675840 | tf_op jit(solution)/shard_map/all_gather | solution.py:68
  434.1 2.7 gather_fusion.1
  436.9 2.0 select_reduce_fusion
  443.1 6.7 %all-to-all-start.2 = ((f32[32,4,10]{2,1,0:T(4,128)}), f32[32,4,10]{2,1,0:T(4,128)S(1)}, u32[]{:S(2)}, u32[]{:S(2)}) async-start(f32[32,4,10]{2,1,0:T(4,128)} %copy.58), calls=%async_computation.2 | async-start | bytes 131072 | tf_op jit(solution)/shard_map/all_to_all | solution.py:116
  449.8 2.7 convolution_multiply_fusion
  452.4 6.5 %all-to-all-done.2 = f32[32,4,10]{2,1,0:T(4,128)S(1)} async-done(((f32[32,4,10]{2,1,0:T(4,128)}), f32[32,4,10]{2,1,0:T(4,128)S(1)}, u32[]{:S(2)}, u32[]{:S(2)}) %all-to-all-start.2) | async-done | bytes 5152 | tf_op jit(solution)/shard_map/all_to_all | solution.py:116
  458.9 5.0 all-to-all-start
  463.9 2.3 fusion.11
  466.2 1.9 copy.55
  468.1 4.9 all-to-all-done
  473.1 6.7 %all-to-all-start.1 = ((f32[32,4,10,256]{3,1,2,0:T(4,128)}), f32[32,4,10,256]{3,1,2,0:T(4,128)}, u32[]{:S(2)}, u32[]{:S(2)}) async-start(f32[32,4,10,256]{3,1,2,0:T(4,128)} %copy.55), calls=%async_computation.1 | async-start | bytes 2621440 | tf_op jit(solution)/shard_map/all_to_all | solution.py:117
  480.5 18.4 %all-to-all-done.1 = f32[32,4,10,256]{3,1,2,0:T(4,128)} async-done(((f32[32,4,10,256]{3,1,2,0:T(4,128)}), f32[32,4,10,256]{3,1,2,0:T(4,128)}, u32[]{:S(2)}, u32[]{:S(2)}) %all-to-all-start.1) | async-done | bytes 1310752 | tf_op jit(solution)/shard_map/all_to_all | solution.py:117
  500.9 13.3 %all-gather.1 = bf16[8,4,2560]{2,1,0:T(4,128)(2,1)S(1)} all-gather(bf16[1,4,2560]{2,1,0:T(4,128)(2,1)S(1)} %reshape.292), channel_id=1, replica_groups=mesh['seq'=32,'mlp'=8] {'mlp'}, dimensions={0}, use_global_device_ids=true | all-gather | bytes 184320 | tf_op jit(solution)/shard_map/all_gather | solution.py:145
  514.3 2.0 fusion.10
  516.3 12.8 %all-gather.2 = bf16[8,320,32]{1,2,0:T(8,128)(2,1)S(1)} all-gather(bf16[1,320,32]{1,2,0:T(8,128)(2,1)S(1)} %fusion.10), channel_id=1, replica_groups=mesh['seq'=32,'mlp'=8] {'mlp'}, dimensions={0}, use_global_device_ids=true | all-gather | bytes 184320 | tf_op jit(solution)/shard_map/all_gather | solution.py:150
  529.4 2.5 fusion.74
  531.9 3.0 fusion.9
  538.0 8.7 %collective-permute-done.1 = f32[32,2560]{1,0:T(8,128)S(1)} collective-permute-done((f32[32,2560]{1,0:T(8,128)S(1)}, f32[32,2560]{1,0:T(8,128)S(1)}, u32[]{:S(2)}, u32[]{:S(2)}) %collective-permute-start.1) | collective-permute-done | bytes 327712 | tf_op jit(solution)/shard_map/ppermute | solution.py:164
  546.8 2.3 collective-permute-start.2
  549.7 7.8 %collective-permute-done.2 = f32[32,2560]{1,0:T(8,128)S(1)} collective-permute-done((f32[32,2560]{1,0:T(8,128)S(1)}, f32[32,2560]{1,0:T(8,128)S(1)}, u32[]{:S(2)}, u32[]{:S(2)}) %collective-permute-start.2) | collective-permute-done | bytes 327712 | tf_op jit(solution)/shard_map/ppermute | solution.py:164
  558.4 2.6 convolution_convert_fusion
  (62 shorter events, 16.3 us)
Async XLA Ops:
  0.6 531.3 %copy-start = (bf16[480,2560]{1,0:T(8,128)(2,1)S(1)}, bf16[480,2560]{1,0:T(8,128)(2,1)}, u32[]{:S(2)}) copy-start(bf16[480,2560]{1,0:T(8,128)(2,1)} %param.23) | copy-start | bytes 7372804
  443.1 15.8 %all-to-all-start.2 = ((f32[32,4,10]{2,1,0:T(4,128)}), f32[32,4,10]{2,1,0:T(4,128)S(1)}, u32[]{:S(2)}, u32[]{:S(2)}) async-start(f32[32,4,10]{2,1,0:T(4,128)} %copy.58), calls=%async_computation.2 | async-start | bytes 131072 | tf_op jit(solution)/shard_map/all_to_all | solution.py:116
  458.9 14.2 %all-to-all-start = ((f32[32,4,10]{2,1,0:T(4,128)}), f32[32,4,10]{2,1,0:T(4,128)S(1)}, u32[]{:S(2)}, u32[]{:S(2)}) async-start(f32[32,4,10]{2,1,0:T(4,128)} %copy.51), calls=%async_computation | async-start | bytes 131072 | tf_op jit(solution)/shard_map/all_to_all | solution.py:115
  468.1 11.6 %copy-start.1 = (bf16[4,2560]{1,0:T(4,128)(2,1)S(1)}, bf16[4,2560]{1,0:T(4,128)(2,1)}, u32[]{:S(2)}) copy-start(bf16[4,2560]{1,0:T(4,128)(2,1)} %param.13) | copy-start | bytes 61444
  468.1 11.7 %copy-start.5 = (bf16[4,512]{1,0:T(4,128)(2,1)S(1)}, bf16[4,512]{1,0:T(4,128)(2,1)}, u32[]{:S(2)}) copy-start(bf16[4,512]{1,0:T(4,128)(2,1)} %param.14) | copy-start | bytes 12292
  473.1 25.8 %all-to-all-start.1 = ((f32[32,4,10,256]{3,1,2,0:T(4,128)}), f32[32,4,10,256]{3,1,2,0:T(4,128)}, u32[]{:S(2)}, u32[]{:S(2)}) async-start(f32[32,4,10,256]{3,1,2,0:T(4,128)} %copy.55), calls=%async_computation.1 | async-start | bytes 2621440 | tf_op jit(solution)/shard_map/all_to_all | solution.py:117
  479.7 34.5 %copy-start.3 = (bf16[32,320]{1,0:T(8,128)(2,1)S(1)}, bf16[32,320]{1,0:T(8,128)(2,1)}, u32[]{:S(2)}) copy-start(bf16[32,320]{1,0:T(8,128)(2,1)} %param.18) | copy-start | bytes 61444
  514.2 15.2 %copy-start.2 = (f32[2560]{0:T(1024)S(1)}, f32[2560]{0:T(1024)}, u32[]{:S(2)}) copy-start(f32[2560]{0:T(1024)} %param.20) | copy-start | bytes 30724
  534.9 23.5 %copy-start.4 = (f32[2560]{0:T(1024)S(1)}, f32[2560]{0:T(1024)}, u32[]{:S(2)}) copy-start(f32[2560]{0:T(1024)} %param.24) | copy-start | bytes 30724
  534.9 1.7 collective-permute-start
  536.7 10.0 %collective-permute-start.1 = (f32[32,2560]{1,0:T(8,128)S(1)}, f32[32,2560]{1,0:T(8,128)S(1)}, u32[]{:S(2)}, u32[]{:S(2)}) collective-permute-start(f32[32,2560]{1,0:T(8,128)S(1)} %add.137), channel_id=1, source_target_pairs={{0,2},{1,3},{2,0},{3,1},{4,6},{5,7},{6,4},{7,5},{8,10},{9,11},{10,... | collective-permute-start | bytes 983048 | tf_op jit(solution)/shard_map/ppermute | solution.py:164
  546.8 10.7 %collective-permute-start.2 = (f32[32,2560]{1,0:T(8,128)S(1)}, f32[32,2560]{1,0:T(8,128)S(1)}, u32[]{:S(2)}, u32[]{:S(2)}) collective-permute-start(f32[32,2560]{1,0:T(8,128)S(1)} %add.138), channel_id=1, source_target_pairs={{0,4},{1,5},{2,6},{3,7},{4,0},{5,1},{6,2},{7,3},{8,12},{9,13},{10,... | collective-permute-start | bytes 983048 | tf_op jit(solution)/shard_map/ppermute | solution.py:164
